TPU v7x, 32 devices: a whole 2x2x4 slice. The times are simulated.
32 devices in a mesh: streams: 8 (over z, x), tm: 4 (over y, core).
Axes of the slice: x: 2, y: 2, z: 4, core: 2. Of those that a mesh axis runs over, the one named last changes fastest.
Arguments:
- signal: float32 [2, 2097152], P(None, ('streams', 'tm')), parts along dimension 1, may hold values from -6 to 6
- coarse_taps: float32 [16, 64], replicated, may hold values from -1.5 to 1.5
- fine_taps: float32 [12, 512], replicated, may hold values from -1.8 to 1.8
Outputs:
- channelized: float32 [2, 64, 64, 512], P(None, 'tm', 'streams'), parts along dimension 2
There are 8 independent parts, one for each index of `streams`. A program takes and returns all parts, laid end to end along the dimension named above; an argument that names none is the same for every part. Nothing has to cross between parts.
All inputs are finite; a program needn't handle non-finite values.
Results may differ from a plain program's by a relative error of at most 0.00007.
Values sent between devices are 32-bit elements; how exact they have to be, the bound alone decides.
No kernel may reach another device: no remote copies, remote signals or barrier semaphores. Data moves between devices by JAX's collectives and lax.ppermute only.
A program may use at most 320 MiB of HBM per device.

v0:
```python
import math
import jax
import jax.numpy as jnp
from jax import lax
from jax.sharding import PartitionSpec as P

CHANNELS = 64
FINE = 512
TAPS = 16
FINE_TAPS = 12


def from_behind(array, axis, by):
    length = lax.axis_size(axis)
    pairs = [(i, i + by) for i in range(length) if 0 <= i + by < length]
    return lax.ppermute(array, axis, pairs)


def tables(points):
    counter = jnp.arange(points, dtype=jnp.int32)
    product = counter[:, None] * counter[None, :] % points
    angle = product.astype(jnp.float32) * (2.0 * math.pi / points)
    return (jnp.cos(angle), jnp.sin(angle))


def coarse_branches(extended, coarse_taps, length):
    row_count = length // (2 * CHANNELS)
    summed = jnp.zeros((2, row_count, 2 * CHANNELS), jnp.float32)
    for tap_index in range(TAPS):
        offset = (TAPS - 1 - tap_index) * CHANNELS
        segment = extended[:, offset : offset + length].reshape(2, row_count, 2 * CHANNELS)
        summed = summed + segment * jnp.tile(coarse_taps[tap_index], 2)
    return summed.reshape(2, length // CHANNELS, CHANNELS)


def coarse_spectrum(branches, cosine_rows, sine_rows):
    factor = 1.0 / math.sqrt(CHANNELS)
    highest = lax.Precision.HIGHEST
    real_part = (
        jnp.einsum("kp,tp->kt", cosine_rows, branches[0], precision=highest)
        + jnp.einsum("kp,tp->kt", sine_rows, branches[1], precision=highest)
    ) * factor
    imag_part = (
        jnp.einsum("kp,tp->kt", cosine_rows, branches[1], precision=highest)
        - jnp.einsum("kp,tp->kt", sine_rows, branches[0], precision=highest)
    ) * factor
    return jnp.stack([real_part, imag_part])


def fine_section(coarse, fine_taps):
    group_size = coarse.shape[1]
    fine_frames = coarse.shape[2] // FINE
    shaped = coarse.reshape(2, group_size, fine_frames, FINE)
    padded = jnp.pad(shaped, ((0, 0), (0, 0), (FINE_TAPS - 1, 0), (0, 0)))
    summed = jnp.zeros((2, group_size, fine_frames, FINE), jnp.float32)
    for tap_index in range(FINE_TAPS):
        offset = FINE_TAPS - 1 - tap_index
        summed = summed + fine_taps[tap_index] * padded[:, :, offset : offset + fine_frames, :]
    cosine_table, sine_table = tables(FINE)
    factor = 1.0 / math.sqrt(FINE)
    highest = lax.Precision.HIGHEST
    out_real = (
        jnp.matmul(summed[0], cosine_table, precision=highest)
        + jnp.matmul(summed[1], sine_table, precision=highest)
    ) * factor
    out_imag = (
        jnp.matmul(summed[1], cosine_table, precision=highest)
        - jnp.matmul(summed[0], sine_table, precision=highest)
    ) * factor
    return jnp.stack([out_real, out_imag])


def on_device(signal, coarse_taps, fine_taps):
    length = signal.shape[1]
    history = (TAPS - 1) * CHANNELS
    cosine_table, sine_table = tables(CHANNELS)
    previous = from_behind(signal[:, length - history :], "tm", 1)
    extended = jnp.concatenate([previous, signal], axis=1)
    branches = coarse_branches(extended, coarse_taps, length)
    coarse = lax.all_to_all(
        coarse_spectrum(branches, cosine_table, sine_table),
        "tm",
        split_axis=1,
        concat_axis=2,
        tiled=True,
    )
    return fine_section(coarse, fine_taps)


def solution(mesh):
    return jax.shard_map(
        on_device,
        mesh=mesh,
        in_specs=(P(None, ("streams", "tm")), P(), P()),
        out_specs=P(None, "tm", "streams", None),
        check_vma=False,
    )
```

profile of v0, /device:TPU:0, one launch (start us, length us, event | category | flops | bytes accessed | tf_op | source)
XLA Modules:
  0.0 54.4 jit_solution(16357406457331470736)
XLA Ops:
  0.0 0.8 %slice.180 = f32[2,960]{1,0:T(2,128)S(1)} slice(f32[2,65536]{1,0:T(2,128)} %param.3), slice={[0:2], [64576:65536]} | slice | bytes 15360 | tf_op jit(solution)/shard_map/slice | solution.py:77
  0.8 2.4 %collective-permute-start = (f32[2,960]{1,0:T(2,128)S(1)}, f32[2,960]{1,0:T(2,128)S(1)}, u32[]{:S(2)}, u32[]{:S(2)}) collective-permute-start(f32[2,960]{1,0:T(2,128)S(1)} %slice.180), channel_id=1, source_target_pairs={{0,1},{1,2},{2,3},{4,5},{5,6},{6,7},{8,9},{9,10},{10,11},{12,13},{... | collective-permute-start | bytes 23048 | tf_op jit(solution)/shard_map/ppermute | solution.py:16
  3.2 1.0 %slice_bitcast_fusion.21 = (f32[64]{0:T(128)S(1)}, f32[64]{0:T(128)S(1)}, f32[64]{0:T(128)S(1)}, f32[64]{0:T(128)S(1)}, f32[64]{0:T(128)S(1)}, /*index=5*/f32[64...) fusion(f32[16,64]{1,0:T(8,128)} %param.4), kind=kLoop, calls=%fused_computation.166 | loop fusion | bytes 8192 | tf_op jit(solution)/shard_map/tile | solution.py:32
  5.6 4.7 %fusion.23 = (f32[1,2,512,128]{3,1,2,0:T(2,128)S(1)}, f32[1,2,512,128]{3,1,2,0:T(2,128)S(1)}, f32[1,2,512,128]{3,1,2,0:T(2,128)S(1)}, f32[1,2,512,128]{3,1,2,0:T...) fusion(f32[2,960]{1,0:T(2,128)S(1)} %collective-permute-done, f32[2,65536]{1,0:T(2,128)} %param.3), kind=kLoop, calls=%fused_computation.51 | loop fusion | flops 786432 | bytes 3677696
  10.3 2.6 %fusion.35 = (f32[1,2,512,128]{3,1,2,0:T(2,128)S(1)}, f32[1,2,512,128]{3,1,2,0:T(2,128)S(1)}, f32[1,2,512,128]{3,1,2,0:T(2,128)S(1)}, f32[1,2,512,128]{3,1,2,0:T...) fusion(f32[2,960]{1,0:T(2,128)S(1)} %collective-permute-done, f32[2,65536]{1,0:T(2,128)S(1)} %copy-done), kind=kLoop, calls=%fused_computation.63 | loop fusion | flops 786432 | bytes 3677696
  12.9 1.3 %fusion.47 = (f32[1,2,512,128]{3,1,2,0:T(2,128)S(1)}, f32[1,2,512,128]{3,1,2,0:T(2,128)S(1)}, f32[1,2,512,128]{3,1,2,0:T(2,128)S(1)}) fusion(f32[2,960]{1,0:T(2,128)S(1)} %collective-permute-done, f32[2,65536]{1,0:T(2,128)S(1)} %copy-done), kind=kLoop, calls=%fused_computation.75 | loop fusion | flops 393216 | bytes 2104832
  14.2 0.6 %fusion.66 = f32[2,512,128]{2,1,0:T(8,128)S(1)} fusion(f32[1,2,512,128]{3,1,2,0:T(2,128)S(1)} %get-tuple-element.18, f32[1,2,512,128]{3,1,2,0:T(2,128)S(1)} %get-tuple-element.19, f32[1,2,512,128]{3,1,2,0:T(2,128)S(1)} %get-tuple-element.17, f32[1,2,512,128]{3,1,2,0:T(2,128)S(1)} %get-tuple-element.16, f32[1,2,512,128]{3,1,2,0:T(2,128)S(1)} %get-tuple-element.15, ...), kind=kLoop, calls=%fused_computation.95 | loop fusion | flops 4063232 | bytes 8921088 | tf_op jit(solution)/shard_map/add | solution.py:32
  14.8 0.1 squeeze.16
  15.0 0.8 %fusion.98 = f32[64,1024]{1,0:T(8,128)S(1)} fusion(f32[1024,64]{1,0:T(8,128)S(1)} %squeeze.16), kind=kOutput, calls=%fused_computation.146 | convolution fusion | flops 50388992 | bytes 524288 | tf_op jit(solution)/shard_map/kp,tp->kt/dot_general | solution.py:40
  15.8 0.2 squeeze.17
  15.9 0.8 %fusion.96 = f32[64,1024]{1,0:T(8,128)S(1)} fusion(f32[1024,64]{1,0:T(8,128)S(1)} %squeeze.17), kind=kOutput, calls=%fused_computation.145 | convolution fusion | flops 50388992 | bytes 524288 | tf_op jit(solution)/shard_map/kp,tp->kt/dot_general | solution.py:44
  16.7 0.8 %fusion.3 = f32[1,64,1024]{2,1,0:T(8,128)S(1)} fusion(f32[64,1024]{1,0:T(8,128)S(1)} %fusion.98, f32[1024,64]{1,0:T(8,128)S(1)} %squeeze.17), kind=kOutput, calls=%fused_computation.29 | convolution fusion | flops 50520064 | bytes 786432 | tf_op jit(solution)/shard_map/kp,tp->kt/dot_general | solution.py:41
  17.5 0.8 %fusion.1 = f32[1,64,1024]{2,1,0:T(8,128)S(1)} fusion(f32[64,1024]{1,0:T(8,128)S(1)} %fusion.96, f32[1024,64]{1,0:T(8,128)S(1)} %squeeze.16), kind=kOutput, calls=%fused_computation.26 | convolution fusion | flops 50520064 | bytes 786432 | tf_op jit(solution)/shard_map/kp,tp->kt/dot_general | solution.py:45
  18.4 1.2 %copy.6 = f32[2,64,1024]{2,0,1:T(2,128)} copy(f32[2,64,1024]{2,1,0:T(8,128)S(1)} %pad_maximum_fusion.1) | data formatting | bytes 1048576 | tf_op jit(solution)/shard_map/stack | solution.py:47
  19.6 4.5 %all-to-all-start = ((f32[2,64,1024]{2,0,1:T(2,128)}), f32[2,64,1024]{2,0,1:T(2,128)S(1)}, u32[]{:S(2)}, u32[]{:S(2)}) async-start(f32[2,64,1024]{2,0,1:T(2,128)} %copy.6), calls=%async_computation | async-start | bytes 1048576 | tf_op jit(solution)/shard_map/all_to_all | solution.py:80
  24.1 8.8 %all-to-all-done = f32[2,64,1024]{2,0,1:T(2,128)S(1)} async-done(((f32[2,64,1024]{2,0,1:T(2,128)}), f32[2,64,1024]{2,0,1:T(2,128)S(1)}, u32[]{:S(2)}, u32[]{:S(2)}) %all-to-all-start) | async-done | bytes 524320 | tf_op jit(solution)/shard_map/all_to_all | solution.py:80
  32.9 0.3 copy.41
  33.3 0.2 reshape.109
  33.5 0.6 %fusion.59 = f32[2,16,8,512]{3,2,1,0:T(8,128)S(1)} fusion(f32[2,16,8,512]{3,2,1,0:T(8,128)S(1)} %reshape.109, f32[512]{0:T(512)S(1)} %bitcast.214, f32[512]{0:T(512)S(1)} %bitcast.215, f32[512]{0:T(512)S(1)} %bitcast.205, f32[512]{0:T(512)S(1)} %bitcast.206, f32[512]{0:T(512)S(1)} %bitcast.207, f32[512]{0:T(512)S(1)} %bitcast.208, f32[512]{0:T(512)S(1)} %bitcast.209, ...), kind=kLoop, calls=%fused_computation.87 | loop fusion | flops 2490368 | bytes 1073152 | tf_op jit(solution)/shard_map/add | solution.py:58
  34.1 4.9 %fusion.15 = f32[16,8,512]{2,1,0:T(8,128)S(1)} fusion(f32[2,16,8,512]{3,2,1,0:T(8,128)S(1)} %fusion.59), kind=kOutput, calls=%fused_computation.43 | convolution fusion | flops 406323200 | bytes 524288 | tf_op jit(solution)/shard_map/dot_general | solution.py:63
  39.0 4.9 %fusion.13 = f32[16,8,512]{2,1,0:T(8,128)S(1)} fusion(f32[2,16,8,512]{3,2,1,0:T(8,128)S(1)} %fusion.59), kind=kOutput, calls=%fused_computation.41 | convolution fusion | flops 406323200 | bytes 524288 | tf_op jit(solution)/shard_map/dot_general | solution.py:67
  43.8 4.9 %fusion.7 = f32[1,16,8,512]{3,2,1,0:T(8,128)S(1)} fusion(f32[16,8,512]{2,1,0:T(8,128)S(1)} %fusion.15, f32[2,16,8,512]{3,2,1,0:T(8,128)S(1)} %fusion.59), kind=kOutput, calls=%fused_computation.35 | convolution fusion | flops 406454272 | bytes 786432 | tf_op jit(solution)/shard_map/dot_general | solution.py:64
  48.7 4.9 %fusion.5 = f32[1,16,8,512]{3,2,1,0:T(8,128)S(1)} fusion(f32[16,8,512]{2,1,0:T(8,128)S(1)} %fusion.13, f32[2,16,8,512]{3,2,1,0:T(8,128)S(1)} %fusion.59), kind=kOutput, calls=%fused_computation.32 | convolution fusion | flops 406454272 | bytes 786432 | tf_op jit(solution)/shard_map/dot_general | solution.py:68
  53.6 0.8 %pad_maximum_fusion.2 = f32[2,16,8,512]{3,2,1,0:T(8,128)} fusion(f32[1,16,8,512]{3,2,1,0:T(8,128)S(1)} %fusion.5, f32[1,16,8,512]{3,2,1,0:T(8,128)S(1)} %fusion.7), kind=kLoop, calls=%fused_computation.128 | loop fusion | flops 131072 | bytes 1048576 | tf_op jit(solution)/shard_map/stack | solution.py:70
  (40 shorter events, 1.5 us)
Async XLA Ops:
  0.8 4.8 %collective-permute-start = (f32[2,960]{1,0:T(2,128)S(1)}, f32[2,960]{1,0:T(2,128)S(1)}, u32[]{:S(2)}, u32[]{:S(2)}) collective-permute-start(f32[2,960]{1,0:T(2,128)S(1)} %slice.180), channel_id=1, source_target_pairs={{0,1},{1,2},{2,3},{4,5},{5,6},{6,7},{8,9},{9,10},{10,11},{12,13},{... | collective-permute-start | bytes 23048 | tf_op jit(solution)/shard_map/ppermute | solution.py:16
  5.6 4.7 %copy-start = (f32[2,65536]{1,0:T(2,128)S(1)}, f32[2,65536]{1,0:T(2,128)}, u32[]{:S(2)}) copy-start(f32[2,65536]{1,0:T(2,128)} %param.3) | copy-start | bytes 1572868
  19.6 4.5 %copy-start.1 = (f32[12,512]{1,0:T(8,128)S(1)}, f32[12,512]{1,0:T(8,128)}, u32[]{:S(2)}) copy-start(f32[12,512]{1,0:T(8,128)} %param.5) | copy-start | bytes 73732
  19.6 13.3 %all-to-all-start = ((f32[2,64,1024]{2,0,1:T(2,128)}), f32[2,64,1024]{2,0,1:T(2,128)S(1)}, u32[]{:S(2)}, u32[]{:S(2)}) async-start(f32[2,64,1024]{2,0,1:T(2,128)} %copy.6), calls=%async_computation | async-start | bytes 1048576 | tf_op jit(solution)/shard_map/all_to_all | solution.py:80
where the time goes:
time: 54.7 us; the launch traced here: 54.4 us
  matrix products  22.7 us (41%)
  other arithmetic  10.6 us (19%)
  waiting for transfers between devices  8.79 us (16%)
  starting transfers between devices  6.89 us (13%)
  local copies, waits for them, and re-layouts  5.27 us (10%)
    all_to_all x1, waiting for transfers between devices, on_device(): lax.all_to_all(coarse_spectrum(branches, cosine_table, sine_table), 'tm',...  8.79 us
    unnamed x3, other arithmetic  8.52 us
    dot_general x1, matrix products, fine_section(): jnp.matmul(summed[0], cosine_table, precision=highest)  4.87 us
    dot_general x1, matrix products, fine_section(): jnp.matmul(summed[1], cosine_table, precision=highest)  4.87 us
    dot_general x1, matrix products, fine_section(): jnp.matmul(summed[0], sine_table, precision=highest)  4.86 us
    dot_general x1, matrix products, fine_section(): jnp.matmul(summed[1], sine_table, precision=highest)  4.86 us
    all_to_all x1, starting transfers between devices, on_device(): lax.all_to_all(coarse_spectrum(branches, cosine_table, sine_table), 'tm',...  4.5 us
    ppermute x1, starting transfers between devices, from_behind(): return lax.ppermute(array, axis, pairs)  2.39 us
  transfers between devices with their start and end apart: 2, of which 1 were waited for; matrix products, arithmetic and copies ran while one was open for 4% of the time, Pallas kernels for 0%

commit v1 on v0

--- a/solution.py
+++ b/solution.py
@@ -8,6 +8,18 @@
 FINE = 512
 TAPS = 16
 FINE_TAPS = 12
+
+
+def cut_along(x, dim, size):
+    lengths = x.shape
+    blocks = x.reshape(*lengths[:dim], size, lengths[dim] // size, *lengths[dim + 1 :])
+    return jnp.moveaxis(blocks, dim, 0)
+
+
+def laid_out(tiles, dim):
+    shape = list(tiles.shape[1:])
+    shape[dim] *= tiles.shape[0]
+    return jnp.moveaxis(tiles, 0, dim).reshape(shape)
 
 
 def from_behind(array, axis, by):
@@ -77,13 +89,15 @@
     previous = from_behind(signal[:, length - history :], "tm", 1)
     extended = jnp.concatenate([previous, signal], axis=1)
     branches = coarse_branches(extended, coarse_taps, length)
-    coarse = lax.all_to_all(
-        coarse_spectrum(branches, cosine_table, sine_table),
-        "tm",
-        split_axis=1,
-        concat_axis=2,
-        tiled=True,
-    )
+    x = coarse_spectrum(branches, cosine_table, sine_table)
+    size, place = (lax.axis_size("tm"), lax.axis_index("tm"))
+    tiles = cut_along(x, 1, size)
+    outs = [tiles[place]]
+    for step in range(1, size):
+        sent = tiles[(place + step) % size]
+        outs.append(lax.ppermute(sent, "tm", [(i_2, (i_2 + step) % size) for i_2 in range(size)]))
+    tiles = jnp.stack(outs)[(place - jnp.arange(size)) % size]
+    coarse = laid_out(tiles, 2)
     return fine_section(coarse, fine_taps)
 
 

time: 54.7 us -> 50.8 us (0.929)
  waiting for transfers between devices: 8.79 us -> 4.57 us
  other arithmetic: 10.6 us -> 11.7 us
  local copies, waits for them, and re-layouts: 5.27 us -> 4.64 us
    all_to_all x1 -> x0, waiting for transfers between devices: 8.79 us -> none  [on_device(): lax.all_to_all(coarse_spectrum(branches, cosine_table, sine_table), 'tm',...]
    ppermute x0 -> x3, waiting for transfers between devices: none -> 4.56 us  [on_device(): lax.ppermute(sent, 'tm', [(i_2, (i_2 + step) % size) for i_2 in range(siz...]
    all_to_all x1 -> x0, starting transfers between devices: 4.5 us -> none  [on_device(): lax.all_to_all(coarse_spectrum(branches, cosine_table, sine_table), 'tm',...]
    ppermute x0 -> x3, starting transfers between devices: none -> 4.11 us  [on_device(): lax.ppermute(sent, 'tm', [(i_2, (i_2 + step) % size) for i_2 in range(siz...]
    slice x1, other arithmetic: 0.02 us -> 1.04 us  [fine_section(): fine_taps[tap_index] * padded[:, :, offset:offset + fine_frames, :]]
    another operation x1, local copies, waits for them, and re-layouts: 1.2 us -> 0.21 us  [fine_section(): shaped = coarse.reshape(2, group_size, fine_frames, FINE)]
    gather x0 -> x1, local copies, waits for them, and re-layouts: none -> 0.58 us  [on_device(): tiles = jnp.stack(outs)[(place - jnp.arange(size)) % size]]
  transfers between devices with their start and end apart: 2 -> 4, of which waited for: 1 -> 3; matrix products, arithmetic and copies ran while one was open for 4% -> 7% of each run, Pallas kernels for 0% -> 0%
where the time goes in v1:
time: 50.8 us; the launch traced here: 50.3 us
  matrix products  22.7 us (45%)
  other arithmetic  11.7 us (23%)
  starting transfers between devices  6.5 us (13%)
  local copies, waits for them, and re-layouts  4.64 us (9%)
  waiting for transfers between devices  4.57 us (9%)
    unnamed x3, other arithmetic  8.52 us
    dot_general x1, matrix products, fine_section(): jnp.matmul(summed[1], cosine_table, precision=highest)  4.87 us
    dot_general x1, matrix products, fine_section(): jnp.matmul(summed[0], cosine_table, precision=highest)  4.87 us
    dot_general x1, matrix products, fine_section(): jnp.matmul(summed[0], sine_table, precision=highest)  4.86 us
    dot_general x1, matrix products, fine_section(): jnp.matmul(summed[1], sine_table, precision=highest)  4.86 us
    ppermute x3, waiting for transfers between devices, on_device(): lax.ppermute(sent, 'tm', [(i_2, (i_2 + step) % size) for i_2 in range(siz...  4.56 us
    ppermute x3, starting transfers between devices, on_device(): lax.ppermute(sent, 'tm', [(i_2, (i_2 + step) % size) for i_2 in range(siz...  4.11 us
    ppermute x1, starting transfers between devices, from_behind(): return lax.ppermute(array, axis, pairs)  2.39 us
  transfers between devices with their start and end apart: 4, of which 3 were waited for; matrix products, arithmetic and copies ran while one was open for 7% of the time, Pallas kernels for 0%

profile of v1, /device:TPU:0, one launch (start us, length us, event | category | flops | bytes accessed | tf_op | source)
XLA Modules:
  0.0 50.3 jit_solution(16801210844590410831)
XLA Ops:
  0.0 0.8 %slice.180 = f32[2,960]{1,0:T(2,128)S(1)} slice(f32[2,65536]{1,0:T(2,128)} %param.3), slice={[0:2], [64576:65536]} | slice | bytes 15360 | tf_op jit(solution)/shard_map/slice | solution.py:89
  0.8 2.4 %collective-permute-start = (f32[2,960]{1,0:T(2,128)S(1)}, f32[2,960]{1,0:T(2,128)S(1)}, u32[]{:S(2)}, u32[]{:S(2)}) collective-permute-start(f32[2,960]{1,0:T(2,128)S(1)} %slice.180), channel_id=1, source_target_pairs={{0,1},{1,2},{2,3},{4,5},{5,6},{6,7},{8,9},{9,10},{10,11},{12,13},{... | collective-permute-start | bytes 23048 | tf_op jit(solution)/shard_map/ppermute | solution.py:28
  3.2 1.0 %fusion.143 = (f32[1,512]{1,0:T(1,128)S(1)}, f32[1,512]{1,0:T(1,128)S(1)}, f32[1,512]{1,0:T(1,128)S(1)}, f32[1,512]{1,0:T(1,128)S(1)}, f32[1,512]{1,0:T(1,128)S(...) fusion(f32[12,512]{1,0:T(8,128)} %param.5), kind=kLoop, calls=%fused_computation.221 | loop fusion | flops 2048 | bytes 49152 | tf_op jit(solution)/shard_map/slice | solution.py:70
  4.2 1.0 %slice_bitcast_fusion.21 = (f32[64]{0:T(128)S(1)}, f32[64]{0:T(128)S(1)}, f32[64]{0:T(128)S(1)}, f32[64]{0:T(128)S(1)}, f32[64]{0:T(128)S(1)}, /*index=5*/f32[64...) fusion(f32[16,64]{1,0:T(8,128)} %param.4), kind=kLoop, calls=%fused_computation.195 | loop fusion | bytes 8192 | tf_op jit(solution)/shard_map/tile | solution.py:44
  6.7 4.7 %fusion.21 = (f32[1,2,512,128]{3,1,2,0:T(2,128)S(1)}, f32[1,2,512,128]{3,1,2,0:T(2,128)S(1)}, f32[1,2,512,128]{3,1,2,0:T(2,128)S(1)}, f32[1,2,512,128]{3,1,2,0:T...) fusion(f32[2,960]{1,0:T(2,128)S(1)} %collective-permute-done, f32[2,65536]{1,0:T(2,128)} %param.3), kind=kLoop, calls=%fused_computation.58 | loop fusion | flops 786432 | bytes 3677696
  11.4 2.6 %fusion.33 = (f32[1,2,512,128]{3,1,2,0:T(2,128)S(1)}, f32[1,2,512,128]{3,1,2,0:T(2,128)S(1)}, f32[1,2,512,128]{3,1,2,0:T(2,128)S(1)}, f32[1,2,512,128]{3,1,2,0:T...) fusion(f32[2,960]{1,0:T(2,128)S(1)} %collective-permute-done, f32[2,65536]{1,0:T(2,128)S(1)} %copy-done), kind=kLoop, calls=%fused_computation.70 | loop fusion | flops 786432 | bytes 3677696
  14.0 1.3 %fusion.45 = (f32[1,2,512,128]{3,1,2,0:T(2,128)S(1)}, f32[1,2,512,128]{3,1,2,0:T(2,128)S(1)}, f32[1,2,512,128]{3,1,2,0:T(2,128)S(1)}) fusion(f32[2,960]{1,0:T(2,128)S(1)} %collective-permute-done, f32[2,65536]{1,0:T(2,128)S(1)} %copy-done), kind=kLoop, calls=%fused_computation.82 | loop fusion | flops 393216 | bytes 2104832
  15.2 0.6 %fusion.64 = f32[2,512,128]{2,1,0:T(8,128)S(1)} fusion(f32[1,2,512,128]{3,1,2,0:T(2,128)S(1)} %get-tuple-element.18, f32[1,2,512,128]{3,1,2,0:T(2,128)S(1)} %get-tuple-element.19, f32[1,2,512,128]{3,1,2,0:T(2,128)S(1)} %get-tuple-element.17, f32[1,2,512,128]{3,1,2,0:T(2,128)S(1)} %get-tuple-element.16, f32[1,2,512,128]{3,1,2,0:T(2,128)S(1)} %get-tuple-element.15, ...), kind=kLoop, calls=%fused_computation.102 | loop fusion | flops 4063232 | bytes 8921088 | tf_op jit(solution)/shard_map/add | solution.py:44
  16.0 0.8 %fusion.102 = f32[64,1024]{1,0:T(8,128)S(1)} fusion(f32[1024,64]{1,0:T(8,128)S(1)} %squeeze.26), kind=kOutput, calls=%fused_computation.159 | convolution fusion | flops 50388992 | bytes 524288 | tf_op jit(solution)/shard_map/kp,tp->kt/dot_general | solution.py:56
  17.0 0.8 %fusion.104 = f32[64,1024]{1,0:T(8,128)S(1)} fusion(f32[1024,64]{1,0:T(8,128)S(1)} %squeeze.25), kind=kOutput, calls=%fused_computation.160 | convolution fusion | flops 50388992 | bytes 524288 | tf_op jit(solution)/shard_map/kp,tp->kt/dot_general | solution.py:52
  17.8 0.8 %fusion = f32[64,1024]{1,0:T(8,128)S(1)} fusion(f32[64,1024]{1,0:T(8,128)S(1)} %fusion.102, f32[1024,64]{1,0:T(8,128)S(1)} %squeeze.25), kind=kOutput, calls=%fused_computation.26 | convolution fusion | flops 50520064 | bytes 786432 | tf_op jit(solution)/shard_map/kp,tp->kt/dot_general | solution.py:57
  18.6 0.8 %fusion.1 = f32[64,1024]{1,0:T(8,128)S(1)} fusion(f32[64,1024]{1,0:T(8,128)S(1)} %fusion.104, f32[1024,64]{1,0:T(8,128)S(1)} %squeeze.26), kind=kOutput, calls=%fused_computation.28 | convolution fusion | flops 50520064 | bytes 786432 | tf_op jit(solution)/shard_map/kp,tp->kt/dot_general | solution.py:53
  19.5 2.7 %collective-permute-start.1 = (f32[2,16,1024]{2,1,0:T(8,128)S(1)}, f32[2,16,1024]{2,1,0:T(8,128)S(1)}, u32[]{:S(2)}, u32[]{:S(2)}) collective-permute-start(f32[2,16,1024]{2,1,0:T(8,128)S(1)} %get-tuple-element.21), channel_id=1, source_target_pairs={{0,1},{1,2},{2,3},{3,0},{4,5},{5,6},{6,7},{7,4},{8,9},{9,10},{10,1... | collective-permute-start | bytes 393224 | tf_op jit(solution)/shard_map/ppermute | solution.py:98
  22.2 1.4 %collective-permute-start.3 = (f32[2,16,1024]{2,1,0:T(8,128)S(1)}, f32[2,16,1024]{2,1,0:T(8,128)S(1)}, u32[]{:S(2)}, u32[]{:S(2)}) collective-permute-start(f32[2,16,1024]{2,1,0:T(8,128)S(1)} %get-tuple-element.23), channel_id=1, source_target_pairs={{0,3},{1,0},{2,1},{3,2},{4,7},{5,4},{6,5},{7,6},{8,11},{9,8},{10,9... | collective-permute-start | bytes 393224 | tf_op jit(solution)/shard_map/ppermute | solution.py:98
  23.9 3.7 %collective-permute-done.2 = f32[2,16,1024]{2,1,0:T(8,128)S(1)} collective-permute-done((f32[2,16,1024]{2,1,0:T(8,128)S(1)}, f32[2,16,1024]{2,1,0:T(8,128)S(1)}, u32[]{:S(2)}, u32[]{:S(2)}) %collective-permute-start.2) | collective-permute-done | bytes 131104 | tf_op jit(solution)/shard_map/ppermute | solution.py:98
  27.7 0.5 %collective-permute-done.3 = f32[2,16,1024]{2,1,0:T(8,128)S(1)} collective-permute-done((f32[2,16,1024]{2,1,0:T(8,128)S(1)}, f32[2,16,1024]{2,1,0:T(8,128)S(1)}, u32[]{:S(2)}, u32[]{:S(2)}) %collective-permute-start.3) | collective-permute-done | bytes 131104 | tf_op jit(solution)/shard_map/ppermute | solution.py:98
  28.3 0.6 %gather_fusion = f32[4,2,16,1024]{3,2,1,0:T(8,128)S(1)} fusion(f32[4,2,16,1024]{3,2,1,0:T(8,128)S(1)} %pad_maximum_fusion.1, s32[1024]{0:T(1024)S(1)} %pad_clamp_fusion), kind=kCustom, calls=%fused_computation | custom fusion | bytes 1048592 | tf_op jit(solution)/shard_map/gather | solution.py:99
  28.8 0.3 copy.4
  29.4 0.6 %fusion.57 = f32[2,16,8,512]{3,2,1,0:T(8,128)S(1)} fusion(f32[2,16,8,512]{3,2,1,0:T(8,128)S(1)} %reshape_reshape.3, f32[512]{0:T(512)S(1)} %bitcast.226, f32[512]{0:T(512)S(1)} %bitcast.227, f32[512]{0:T(512)S(1)} %bitcast.217, f32[512]{0:T(512)S(1)} %bitcast.218, f32[512]{0:T(512)S(1)} %bitcast.219, f32[512]{0:T(512)S(1)} %bitcast.220, ...), kind=kLoop, calls=%fused_computation.94 | loop fusion | flops 2490368 | bytes 1073152 | tf_op jit(solution)/shard_map/add | solution.py:70
  30.0 4.9 %fusion.13 = f32[16,8,512]{2,1,0:T(8,128)S(1)} fusion(f32[2,16,8,512]{3,2,1,0:T(8,128)S(1)} %fusion.57), kind=kOutput, calls=%fused_computation.42 | convolution fusion | flops 406323200 | bytes 524288 | tf_op jit(solution)/shard_map/dot_general | solution.py:75
  34.9 4.9 %fusion.11 = f32[16,8,512]{2,1,0:T(8,128)S(1)} fusion(f32[2,16,8,512]{3,2,1,0:T(8,128)S(1)} %fusion.57), kind=kOutput, calls=%fused_computation.40 | convolution fusion | flops 406323200 | bytes 524288 | tf_op jit(solution)/shard_map/dot_general | solution.py:79
  39.7 4.9 %fusion.5 = f32[1,16,8,512]{3,2,1,0:T(8,128)S(1)} fusion(f32[16,8,512]{2,1,0:T(8,128)S(1)} %fusion.13, f32[2,16,8,512]{3,2,1,0:T(8,128)S(1)} %fusion.57), kind=kOutput, calls=%fused_computation.34 | convolution fusion | flops 406454272 | bytes 786432 | tf_op jit(solution)/shard_map/dot_general | solution.py:76
  44.6 4.9 %fusion.3 = f32[1,16,8,512]{3,2,1,0:T(8,128)S(1)} fusion(f32[16,8,512]{2,1,0:T(8,128)S(1)} %fusion.11, f32[2,16,8,512]{3,2,1,0:T(8,128)S(1)} %fusion.57), kind=kOutput, calls=%fused_computation.31 | convolution fusion | flops 406454272 | bytes 786432 | tf_op jit(solution)/shard_map/dot_general | solution.py:80
  49.5 0.8 %pad_maximum_fusion.2 = f32[2,16,8,512]{3,2,1,0:T(8,128)} fusion(f32[1,16,8,512]{3,2,1,0:T(8,128)S(1)} %fusion.3, f32[1,16,8,512]{3,2,1,0:T(8,128)S(1)} %fusion.5), kind=kLoop, calls=%fused_computation.135 | loop fusion | flops 131072 | bytes 1048576 | tf_op jit(solution)/shard_map/stack | solution.py:82
  (45 shorter events, 2.3 us)
Async XLA Ops:
  0.8 5.9 %collective-permute-start = (f32[2,960]{1,0:T(2,128)S(1)}, f32[2,960]{1,0:T(2,128)S(1)}, u32[]{:S(2)}, u32[]{:S(2)}) collective-permute-start(f32[2,960]{1,0:T(2,128)S(1)} %slice.180), channel_id=1, source_target_pairs={{0,1},{1,2},{2,3},{4,5},{5,6},{6,7},{8,9},{9,10},{10,11},{12,13},{... | collective-permute-start | bytes 23048 | tf_op jit(solution)/shard_map/ppermute | solution.py:28
  6.7 4.7 %copy-start = (f32[2,65536]{1,0:T(2,128)S(1)}, f32[2,65536]{1,0:T(2,128)}, u32[]{:S(2)}) copy-start(f32[2,65536]{1,0:T(2,128)} %param.3) | copy-start | bytes 1572868
  19.5 4.4 %collective-permute-start.1 = (f32[2,16,1024]{2,1,0:T(8,128)S(1)}, f32[2,16,1024]{2,1,0:T(8,128)S(1)}, u32[]{:S(2)}, u32[]{:S(2)}) collective-permute-start(f32[2,16,1024]{2,1,0:T(8,128)S(1)} %get-tuple-element.21), channel_id=1, source_target_pairs={{0,1},{1,2},{2,3},{3,0},{4,5},{5,6},{6,7},{7,4},{8,9},{9,10},{10,1... | collective-permute-start | bytes 393224 | tf_op jit(solution)/shard_map/ppermute | solution.py:98
  22.2 5.5 %collective-permute-start.2 = (f32[2,16,1024]{2,1,0:T(8,128)S(1)}, f32[2,16,1024]{2,1,0:T(8,128)S(1)}, u32[]{:S(2)}, u32[]{:S(2)}) collective-permute-start(f32[2,16,1024]{2,1,0:T(8,128)S(1)} %get-tuple-element.22), channel_id=1, source_target_pairs={{0,2},{1,3},{2,0},{3,1},{4,6},{5,7},{6,4},{7,5},{8,10},{9,11},{10,... | collective-permute-start | bytes 393224 | tf_op jit(solution)/shard_map/ppermute | solution.py:98
  22.2 6.0 %collective-permute-start.3 = (f32[2,16,1024]{2,1,0:T(8,128)S(1)}, f32[2,16,1024]{2,1,0:T(8,128)S(1)}, u32[]{:S(2)}, u32[]{:S(2)}) collective-permute-start(f32[2,16,1024]{2,1,0:T(8,128)S(1)} %get-tuple-element.23), channel_id=1, source_target_pairs={{0,3},{1,0},{2,1},{3,2},{4,7},{5,4},{6,5},{7,6},{8,11},{9,8},{10,9... | collective-permute-start | bytes 393224 | tf_op jit(solution)/shard_map/ppermute | solution.py:98
